TPU v7x, 256 devices: a whole 4x4x8 slice. The times are simulated.
256 devices in a mesh: dp: 2 (over x_hi), tm: 16 (over z, x_lo), mp: 8 (over y, core).
Axes of the slice: x: 4 (x_hi: 2, x_lo: 2; x = x_hi * 2 + x_lo), y: 4, z: 8, core: 2. Of those that a mesh axis runs over, the one named last changes fastest.
Arguments:
- features: bfloat16 [128, 576, 1024], P(('dp', 'tm'), 'mp'), parts along dimension 0, may hold values from -6 to 6
- queries: bfloat16 [8192, 1024], P(('dp', 'tm')), parts along dimension 0, may hold values from -6 to 6
- anchor_frame: int32 [8192], P(('dp', 'tm')), parts along dimension 0, may hold values from 0 to 63, as said below
- anchor_patch: int32 [8192], P(('dp', 'tm')), parts along dimension 0, may hold values from 0 to 575
- time_offset: float32 [8192, 8, 4], P(('dp', 'tm')), parts along dimension 0, may hold values from -1.99 to 1.99
- space_offset: float32 [2, 8192, 8, 4], P(None, ('dp', 'tm')), parts along dimension 1, may hold values from -3 to 3
- value_weight: bfloat16 [1024, 1024], replicated, may hold values from -0.1875 to 0.1875
- point_weight: bfloat16 [1024, 32], replicated, may hold values from -0.1875 to 0.1875
- point_bias: float32 [32], replicated, may hold values from -6 to 260
- output_weight: bfloat16 [1024, 1024], P('mp'), may hold values from -0.1875 to 0.1875
- project_weight: bfloat16 [1024, 3584], P(None, 'mp'), may hold values from -2 to 2
- norm_gain: float32 [3584], P('mp'), may hold values from 0.1 to 1.9
- query_weight: bfloat16 [3584, 3072], P(None, 'mp'), may hold values from -0.09375 to 0.09375
- query_bias: float32 [3072], P('mp'), may hold values from -6 to 40
- cache_weight: bfloat16 [3584, 1024], P(None, 'mp'), may hold values from -0.09375 to 0.09375
- cache_bias: float32 [1024], P('mp'), may hold values from -6 to 40
Outputs:
- attention: bfloat16 [8192, 3072], P(('dp', 'tm'), 'mp'), parts along dimension 0
- key_value: bfloat16 [8192, 1024], P(('dp', 'tm'), 'mp'), parts along dimension 0
There are 2 independent parts, one for each index of `dp`. A program takes and returns all parts, laid end to end along the dimension named above; an argument that names none is the same for every part. Nothing has to cross between parts.
Inputs may be any that keep to these rules, and one draw needn't show every extreme that they name: `anchor_frame`: the anchor frame of query q lies among the 4 frames that begin at (q // 256) * 4.
All inputs are finite; a program needn't handle non-finite values.
Results may differ from a plain program's by a relative error of at most 0.04.
Values may be sent and summed in bfloat16 or wider, within the bound.
No kernel may reach another device: no remote copies, remote signals or barrier semaphores. Data moves between devices by JAX's collectives and lax.ppermute only.
A program may use at most 64 MiB of HBM per device.

v0:
```python
import jax
import jax.numpy as jnp
from jax import lax
from jax.sharding import Mesh
from jax.sharding import PartitionSpec as P

AH = 8
POINTS = 4
GRID = 24
KVH = 4
HD = 128
GROUP = 7
MP = ("mp_0", "mp_1")
rope_base = 1000000.0
epsilon = 1e-06
masked = -1e30


def with_halo(block, sides, width):
    for axis, dim in sides:
        count = lax.axis_size(axis)
        forward = [(i, i + 1) for i in range(count - 1)]
        backward = [(target, source) for source, target in forward]
        low = lax.ppermute(
            lax.slice_in_dim(block, block.shape[dim] - width, None, axis=dim), axis, forward
        )
        high = lax.ppermute(lax.slice_in_dim(block, 0, width, axis=dim), axis, backward)
        block = jnp.concatenate([low, block, high], axis=dim)
    return block


def gathered_total(x, axis):
    return lax.all_gather(x, axis).sum(0)


def sent_to_all(x, axis):
    copies = jnp.broadcast_to(x, (lax.axis_size(axis), *x.shape))
    return lax.all_to_all(copies, axis, split_axis=0, concat_axis=0, tiled=True)


def of_everyone(x, axis):
    return sent_to_all(x, axis).sum(axis=0)


def in_order(parts, dim):
    lengths = list(parts.shape[1:])
    lengths[dim] *= parts.shape[0]
    return jnp.moveaxis(parts, 0, dim).reshape(lengths)


def stacked_from(x, axes, sequence):
    parts = x
    for k in sequence:
        parts = lax.all_gather(parts, axes[k])
    done = sequence[::-1]
    back = [done.index(k) for k in range(len(axes))]
    parts = parts.transpose(*back, *range(len(axes), parts.ndim))
    return parts.reshape(-1, *x.shape)


def gather_axes(x, axes, sequence, dim):
    return in_order(stacked_from(x, axes, sequence), dim)


def gather_directly(x, axis, dim):
    return in_order(sent_to_all(x, axis), dim)


def sent_together(arrays, axis, dim, along):
    both = jnp.concatenate(arrays, axis=along)
    out, at, outs = (lax.all_gather(both, axis, axis=dim, tiled=True), 0, [])
    for a in arrays:
        outs.append(lax.slice_in_dim(out, at, at + a.shape[along], axis=along))
        at += a.shape[along]
    return tuple(outs)


def rotate(vectors, positions):
    half_width = vectors.shape[-1] // 2
    frequency = rope_base ** (-2.0 * jnp.arange(half_width, dtype=jnp.float32) / vectors.shape[-1])
    angles = positions.astype(jnp.float32)[:, None] * frequency[None, :]
    cosine = jnp.cos(angles)[:, None, :]
    sine_part = jnp.sin(angles)[:, None, :]
    first_half = vectors[..., :half_width]
    second_half = vectors[..., half_width:]
    return jnp.concatenate(
        [
            first_half * cosine - second_half * sine_part,
            second_half * cosine + first_half * sine_part,
        ],
        axis=-1,
    )


def trilinear_corners(frame_pos, row_pos, column_pos, weight, frame_total, side):
    floor_frame = jnp.floor(frame_pos)
    floor_row = jnp.floor(row_pos)
    floor_column = jnp.floor(column_pos)
    frame_part = frame_pos - floor_frame
    row_part = row_pos - floor_row
    column_part = column_pos - floor_column
    frame_start = floor_frame.astype(jnp.int32)
    row_start = floor_row.astype(jnp.int32)
    column_start = floor_column.astype(jnp.int32)
    listing = []
    for frame_step in (0, 1):
        for row_step in (0, 1):
            for column_step in (0, 1):
                frame_cell = frame_start + frame_step
                row_cell = row_start + row_step
                column_cell = column_start + column_step
                portion = weight * (frame_part if frame_step else 1.0 - frame_part)
                portion = portion * (row_part if row_step else 1.0 - row_part)
                portion = portion * (column_part if column_step else 1.0 - column_part)
                inside = (
                    (frame_cell >= 0)
                    & (frame_cell < frame_total)
                    & (row_cell >= 0)
                    & (row_cell < side)
                )
                inside = inside & (column_cell >= 0) & (column_cell < side)
                portion = jnp.where(inside, portion, 0.0)
                patch_id = jnp.clip(row_cell, 0, side - 1) * side + jnp.clip(
                    column_cell, 0, side - 1
                )
                listing.append((frame_cell, patch_id, portion))
    return listing


def make_attend(query_turned, positions, head_map, scaling):

    def attend(state_in, members, first_row):
        key_rows, value_rows = members
        length = key_rows.shape[0]
        block_len = 512
        block_count = length // block_len
        key_blocks = key_rows.reshape(block_count, block_len, -1, HD)[:, :, head_map, :]
        value_blocks = value_rows.reshape(block_count, block_len, -1, HD)[:, :, head_map, :]
        block_starts = jnp.arange(block_count, dtype=jnp.int32) * block_len

        def advance(running, inputs):
            peak_score, denominator, numerator = running
            key_block, value_block, block_start = inputs
            scores = (
                jnp.einsum(
                    "qhd,nhd->hqn", query_turned, key_block, preferred_element_type=jnp.float32
                )
                * scaling
            )
            key_pos = block_start + jnp.arange(block_len, dtype=jnp.int32)
            allowed = key_pos[None, None, :] <= positions[None, :, None]
            scores = jnp.where(allowed, scores, masked)
            new_peak = jnp.maximum(peak_score, jnp.max(scores, axis=-1))
            weights = jnp.where(allowed, jnp.exp(scores - new_peak[..., None]), 0.0)
            rescale = jnp.exp(peak_score - new_peak)
            denominator = denominator * rescale + jnp.sum(weights, axis=-1)
            numerator = numerator * rescale[..., None] + jnp.einsum(
                "hqn,nhd->hqd",
                weights.astype(jnp.bfloat16),
                value_block,
                preferred_element_type=jnp.float32,
            )
            return ((new_peak, denominator, numerator), None)

        result, unused = lax.scan(advance, state_in, (key_blocks, value_blocks, block_starts))
        return result

    return attend


def local(
    features,
    queries,
    anchor_frame,
    anchor_patch,
    time_offset,
    space_offset,
    value_weight,
    point_weight,
    point_bias,
    output_weight,
    project_weight,
    norm_gain,
    query_weight,
    query_bias,
    cache_weight,
    cache_bias,
):
    groups = lax.axis_size(MP)
    group_index = lax.axis_index(MP)
    frame_index = lax.axis_index("tm")
    frames_here, patches_here, feature_width = features.shape
    rows_here = queries.shape[0]
    frame_total = frames_here * lax.axis_size("tm")
    patch_total = GRID * GRID
    head_width = feature_width // AH
    heads_here = AH // groups
    first_frame = frame_index * frames_here - 2
    projected = jnp.dot(
        features.reshape(frames_here * patches_here, feature_width),
        value_weight,
        preferred_element_type=jnp.float32,
    )
    projected = projected.astype(jnp.bfloat16).reshape(frames_here, patches_here, feature_width)
    logits = jnp.dot(queries, point_weight, preferred_element_type=jnp.float32) + point_bias
    point_share = jax.nn.softmax(logits.reshape(rows_here, AH, POINTS), axis=-1)
    frame_pos = anchor_frame.astype(jnp.float32)[:, None, None] + time_offset
    row_pos = (anchor_patch // GRID).astype(jnp.float32)[:, None, None] + space_offset[0]
    column_pos = (anchor_patch % GRID).astype(jnp.float32)[:, None, None] + space_offset[1]

    def own_slice(array):
        return lax.dynamic_slice_in_dim(array, group_index * heads_here, heads_here, 1)

    by_head = lax.all_to_all(projected, MP, split_axis=2, concat_axis=1, tiled=True)
    padded = with_halo(by_head, (("tm", 0),), 2)
    lookup = padded.reshape(-1, heads_here, head_width)
    head_lane = jnp.arange(heads_here, dtype=jnp.int32)[None, :, None]
    running = jnp.zeros((rows_here, heads_here, head_width), jnp.float32)
    for frame_cell, patch_id, portion in trilinear_corners(
        own_slice(frame_pos),
        own_slice(row_pos),
        own_slice(column_pos),
        own_slice(point_share),
        frame_total,
        GRID,
    ):
        local_frame = jnp.clip(frame_cell - first_frame, 0, frames_here + 3)
        picked = lookup[local_frame * patch_total + patch_id, head_lane]
        running = running + jnp.sum(portion[..., None] * picked.astype(jnp.float32), axis=2)
    sampled = running.reshape(rows_here, heads_here * head_width).astype(jnp.bfloat16)
    head_terms = jnp.dot(sampled, output_weight, preferred_element_type=jnp.float32)
    head_mix = gathered_total(head_terms, MP)
    abstract = (queries.astype(jnp.float32) + head_mix).astype(jnp.bfloat16)
    visual = jnp.dot(abstract, project_weight, preferred_element_type=jnp.float32)
    squares = of_everyone(jnp.sum(visual * visual, axis=1), MP)
    model_width = query_weight.shape[0]
    normed = (visual * lax.rsqrt(squares / model_width + epsilon)[:, None] * norm_gain).astype(
        jnp.bfloat16
    )
    shard_piece = gather_axes(normed, MP, (0, 1), 1)
    query_sum = jnp.dot(shard_piece, query_weight, preferred_element_type=jnp.float32)
    cache_sum = jnp.dot(shard_piece, cache_weight, preferred_element_type=jnp.float32)
    positions = frame_index * rows_here + jnp.arange(rows_here, dtype=jnp.int32)
    query_heads = query_weight.shape[1] // HD
    query_turned = rotate(
        (query_sum + query_bias).reshape(rows_here, query_heads, HD), positions
    ).astype(jnp.bfloat16)
    cache_heads = cache_weight.shape[1] // HD
    cache_state = (cache_sum + cache_bias).reshape(rows_here, cache_heads, HD)
    is_key = group_index * cache_heads + jnp.arange(cache_heads, dtype=jnp.int32) < KVH
    cache_state = jnp.where(is_key[None, :, None], rotate(cache_state, positions), cache_state)
    key_value = cache_state.reshape(rows_here, cache_heads * HD).astype(jnp.bfloat16)
    cache_all = gather_directly(key_value, MP, 1)
    key_rows = cache_all[:, : KVH * HD]
    value_rows = cache_all[:, KVH * HD :]
    own_heads = (group_index * query_heads + jnp.arange(query_heads, dtype=jnp.int32)) // GROUP
    scaling = HD ** (-0.5)
    initial = (
        jnp.full((query_heads, rows_here), masked, jnp.float32),
        jnp.zeros((query_heads, rows_here), jnp.float32),
        jnp.zeros((query_heads, rows_here, HD), jnp.float32),
    )
    span_heads = min(KVH, (query_heads - 1) // GROUP + 2)
    lowest = jnp.minimum(group_index * query_heads // GROUP, KVH - span_heads)
    key_rows = lax.dynamic_slice_in_dim(key_rows, lowest * HD, span_heads * HD, 1)
    value_rows = lax.dynamic_slice_in_dim(value_rows, lowest * HD, span_heads * HD, 1)
    attend = make_attend(query_turned, positions, own_heads - lowest, scaling)
    peak_score, denominator, numerator = attend(
        initial, sent_together((key_rows, value_rows), "tm", 0, 1), jnp.int32(0)
    )
    attention = (
        (numerator / denominator[..., None])
        .transpose(1, 0, 2)
        .reshape(rows_here, query_heads * HD)
        .astype(jnp.bfloat16)
    )
    return (attention, key_value)


def solution(mesh):
    finer = Mesh(
        mesh.devices.reshape(mesh.shape["dp"], mesh.shape["tm"], 4, 2), ("dp", "tm", "mp_0", "mp_1")
    )
    placed = (
        P(("dp", "tm"), MP, None),
        P(("dp", "tm"), None),
        P(("dp", "tm")),
        P(("dp", "tm")),
        P(("dp", "tm"), None, None),
        P(None, ("dp", "tm"), None, None),
        P(),
        P(),
        P(),
        P(MP, None),
        P(None, MP),
        P(MP),
        P(None, MP),
        P(MP),
        P(None, MP),
        P(MP),
    )
    return jax.shard_map(
        local,
        mesh=finer,
        in_specs=placed,
        out_specs=(P(("dp", "tm"), MP), P(("dp", "tm"), MP)),
        check_vma=False,
    )
```

profile of v0, /device:TPU:2, one launch (start us, length us, event | category | flops | bytes accessed | tf_op | source)
XLA Modules:
  0.0 492.8 jit_solution(13112427165565141134)
XLA Ops:
  7.2 3.5 convolution_convert_fusion
  10.7 2.4 copy.159
  13.1 4.6 all-to-all-start
  19.2 14.6 %all-to-all-done = bf16[4,72,1024]{1,0,2:T(4,128)(2,1)} async-done(((bf16[4,72,1024]{1,0,2:T(4,128)(2,1)}), bf16[4,72,1024]{1,0,2:T(4,128)(2,1)}, u32[]{:S(2)}, u32[]{:S(2)}) %all-to-all-start) | async-done | bytes 589856 | tf_op jit(solution)/shard_map/all_to_all | solution.py:214
  33.8 3.5 fusion.75
  37.2 1.9 copy.160
  39.2 3.8 collective-permute-start
  44.0 2.9 collective-permute-start.1
  56.4 2.2 pad_maximum_fusion
  58.6 16.0 %gather_fusion = bf16[1024,128]{1,0:T(8,128)(2,1)} fusion(bf16[4608,1,128]{2,0,1:T(8,128)(2,1)} %bitcast.166, s32[1024]{0:T(1024)S(1)} %reshape.427), kind=kCustom, calls=%fused_computation | custom fusion | bytes 532480 | tf_op jit(solution)/shard_map/gather | solution.py:228
  74.6 16.0 %gather_fusion.1 = bf16[1024,128]{1,0:T(8,128)(2,1)} fusion(bf16[4608,1,128]{2,0,1:T(8,128)(2,1)} %bitcast.167, s32[1024]{0:T(1024)S(1)} %reshape.435), kind=kCustom, calls=%fused_computation.1 | custom fusion | bytes 532480 | tf_op jit(solution)/shard_map/gather | solution.py:228
  90.6 16.0 %gather_fusion.2 = bf16[1024,128]{1,0:T(8,128)(2,1)} fusion(bf16[4608,1,128]{2,0,1:T(8,128)(2,1)} %bitcast.168, s32[1024]{0:T(1024)S(1)} %reshape.443), kind=kCustom, calls=%fused_computation.2 | custom fusion | bytes 532480 | tf_op jit(solution)/shard_map/gather | solution.py:228
  106.6 16.0 %gather_fusion.3 = bf16[1024,128]{1,0:T(8,128)(2,1)} fusion(bf16[4608,1,128]{2,0,1:T(8,128)(2,1)} %bitcast.169, s32[1024]{0:T(1024)S(1)} %reshape.451), kind=kCustom, calls=%fused_computation.3 | custom fusion | bytes 532480 | tf_op jit(solution)/shard_map/gather | solution.py:228
  122.7 15.9 %gather_fusion.4 = bf16[1024,128]{1,0:T(8,128)(2,1)} fusion(bf16[4608,1,128]{2,0,1:T(8,128)(2,1)} %bitcast.170, s32[1024]{0:T(1024)S(1)} %reshape.459), kind=kCustom, calls=%fused_computation.4 | custom fusion | bytes 532480 | tf_op jit(solution)/shard_map/gather | solution.py:228
  138.6 16.0 %gather_fusion.5 = bf16[1024,128]{1,0:T(8,128)(2,1)} fusion(bf16[4608,1,128]{2,0,1:T(8,128)(2,1)} %bitcast.171, s32[1024]{0:T(1024)S(1)} %reshape.467), kind=kCustom, calls=%fused_computation.5 | custom fusion | bytes 532480 | tf_op jit(solution)/shard_map/gather | solution.py:228
  154.6 11.4 %gather_fusion.6 = bf16[1024,128]{1,0:T(8,128)(2,1)S(1)} fusion(bf16[4608,1,128]{2,0,1:T(8,128)(2,1)} %bitcast.172, s32[1024]{0:T(1024)S(1)} %reshape.475), kind=kCustom, calls=%fused_computation.6 | custom fusion | bytes 532480 | tf_op jit(solution)/shard_map/gather | solution.py:228
  165.9 11.4 %gather_fusion.7 = bf16[1024,128]{1,0:T(8,128)(2,1)S(1)} fusion(bf16[4608,1,128]{2,0,1:T(8,128)(2,1)} %bitcast.173, s32[1024]{0:T(1024)S(1)} %reshape.483), kind=kCustom, calls=%fused_computation.7 | custom fusion | bytes 532480 | tf_op jit(solution)/shard_map/gather | solution.py:228
  186.6 55.3 %all-gather.9.cloned.1.call-done = f32[2048,1024]{1,0:T(8,128)} async-done(((f32[256,1024]{1,0:T(8,128)}), f32[2048,1024]{1,0:T(8,128)}) %all-gather.9.cloned.1.call-update) | async-done | bytes 8388624 | tf_op jit(solution)/shard_map/all_gather | solution.py:33
  241.9 5.5 %reduce_sum.126 = f32[256,1024]{1,0:T(8,128)} reduce(f32[8,256,1024]{2,1,0:T(8,128)} %bitcast.176, f32[]{:T(128)} %constant.44.clone.1), dimensions={0}, to_apply=%region_10.11 | reduce | flops 1835008 | bytes 9437188 | tf_op jit(solution)/shard_map/reduce_sum | solution.py:33
  247.4 2.7 multiply_reduce_fusion
  250.1 8.3 %all_to_all.29 = f32[8,1,256]{2,1,0:T(1,128)S(1)} all-to-all(f32[8,1,256]{2,1,0:T(1,128)S(1)} %broadcast_in_dim.123), channel_id=1, replica_groups=mesh['dp'=2,'tm'=16,'mp_0'=4,'mp_1'=2] {'mp_0','mp_1'}, dimensions={0} | all-to-all | bytes 16384 | tf_op jit(solution)/shard_map/all_to_all | solution.py:38
  259.6 14.3 %all-gather.1 = bf16[1024,448]{0,1:T(8,128)(2,1)S(1)} all-gather(bf16[256,448]{0,1:T(8,128)(2,1)S(1)} %multiply_convert_fusion), channel_id=3, replica_groups=mesh['dp'=2,'tm'=16,'mp_0'=4,'mp_1'=2] {'mp_0'}, dimensions={0}, use_global_device_ids=true | all-gather | bytes 1146880 | tf_op jit(solution)/shard_map/all_gather | solution.py:54
  274.9 15.4 %all-gather.11.cloned.1.call-done = bf16[8,256,448]{1,2,0:T(8,128)(2,1)} async-done(((bf16[4,256,448]{1,2,0:T(8,128)(2,1)}), bf16[8,256,448]{1,2,0:T(8,128)(2,1)}) %all-gather.11.cloned.1.call-update) | async-done | bytes 1835024 | tf_op jit(solution)/shard_map/all_gather | solution.py:54
  295.0 4.4 all-to-all-start.2
  299.5 10.3 %all-to-all-done.2 = bf16[8,256,128]{1,2,0:T(8,128)(2,1)S(1)} async-done(((bf16[8,256,128]{1,2,0:T(8,128)(2,1)}), bf16[8,256,128]{1,2,0:T(8,128)(2,1)S(1)}, u32[]{:S(2)}, u32[]{:S(2)}) %all-to-all-start.2) | async-done | bytes 524320 | tf_op jit(solution)/shard_map/all_to_all | solution.py:38
  311.7 3.4 convolution_add_fusion.1
  316.5 113.7 %all-gather.7.cloned.1.call-done = bf16[4096,512]{0,1:T(8,128)(2,1)} async-done(((bf16[256,512]{0,1:T(8,128)(2,1)}), bf16[4096,512]{0,1:T(8,128)(2,1)}) %all-gather.7.cloned.1.call-update) | async-done | bytes 4194320 | tf_op jit(solution)/shard_map/all_gather | solution.py:71
  430.2 2.7 fusion.74
  435.5 2.0 copy.181
  437.5 2.5 gather_fusion.9
  440.0 4.1 gather_fusion.8
  444.1 40.3 %while.15 = (s32[]{:T(128)}, f32[3,256]{1,0:T(4,128)S(1)}, f32[3,256]{1,0:T(4,128)S(1)}, f32[3,256,128]{2,1,0:T(8,128)S(1)}, s32[8]{0:T(128)S(1)}, /*index=5*/bf...) while((s32[]{:T(128)}, f32[3,256]{1,0:T(4,128)S(1)}, ...), condition=%wide.region_16.17_spmd.clone, body=%wide.region_13.16_spmd.clone.sunk | while | flops 205296128 | bytes 7068813 | solution.py:165
  (224 shorter events, 75.0 us)
Async XLA Ops:
  7.2 304.5 %copy-start = (bf16[3584,384]{1,0:T(8,128)(2,1)S(1)}, bf16[3584,384]{1,0:T(8,128)(2,1)}, u32[]{:S(2)}) copy-start(bf16[3584,384]{1,0:T(8,128)(2,1)} %param.30) | copy-start | bytes 8257540
  10.7 7.1 %copy-start.2 = (bf16[256,1024]{1,0:T(8,128)(2,1)S(1)}, bf16[256,1024]{1,0:T(8,128)(2,1)}, u32[]{:S(2)}) copy-start(bf16[256,1024]{1,0:T(8,128)(2,1)} %param.19) | copy-start | bytes 1572868
  10.7 7.1 %copy-start.13 = (bf16[1024,32]{0,1:T(8,128)(2,1)S(1)}, bf16[1024,32]{0,1:T(8,128)(2,1)}, u32[]{:S(2)}) copy-start(bf16[1024,32]{0,1:T(8,128)(2,1)} %param.25) | copy-start | bytes 196612
  10.7 7.1 %copy-start.17 = (f32[32]{0:T(128)S(1)}, f32[32]{0:T(128)}, u32[]{:S(2)}) copy-start(f32[32]{0:T(128)} %param.26) | copy-start | bytes 388
  13.1 5.1 %copy-start.12 = (f32[2,256,8,4]{1,3,2,0:T(4,128)S(1)}, f32[2,256,8,4]{1,3,2,0:T(4,128)}, u32[]{:S(2)}) copy-start(f32[2,256,8,4]{1,3,2,0:T(4,128)} %param.23) | copy-start | bytes 196612
  13.1 5.1 %copy-start.15 = (s32[256]{0:T(256)S(1)}, s32[256]{0:T(256)}, u32[]{:S(2)}) copy-start(s32[256]{0:T(256)} %param.21) | copy-start | bytes 3076
  13.1 5.1 %copy-start.16 = (s32[256]{0:T(256)S(1)}, s32[256]{0:T(256)}, u32[]{:S(2)}) copy-start(s32[256]{0:T(256)} %param.20) | copy-start | bytes 3076
  13.1 20.7 %all-to-all-start = ((bf16[4,72,1024]{1,0,2:T(4,128)(2,1)}), bf16[4,72,1024]{1,0,2:T(4,128)(2,1)}, u32[]{:S(2)}, u32[]{:S(2)}) async-start(bf16[4,72,1024]{1,0,2:T(4,128)(2,1)} %copy.159), calls=%async_computation | async-start | bytes 2097152 | tf_op jit(solution)/shard_map/all_to_all | solution.py:214
  17.7 224.1 %all-gather.9.cloned.1.call-start = ((), (), s32[]{:S(2)}) async-start(), calls=%async_computation.4 | async-start | bytes 9437184 | tf_op jit(solution)/shard_map/all_gather | solution.py:33
  39.2 17.2 %collective-permute-start = (bf16[2,576,128]{2,1,0:T(8,128)(2,1)}, bf16[2,576,128]{2,1,0:T(8,128)(2,1)}, u32[]{:S(2)}, u32[]{:S(2)}) collective-permute-start(bf16[2,576,128]{2,1,0:T(8,128)(2,1)} %bitcast.200), channel_id=1, source_target_pairs={{0,8},{8,16},{16,24},{24,32},{32,40},{40,48},{48,56},{56,64},{64,7... | collective-permute-start | bytes 884744 | tf_op jit(solution)/shard_map/ppermute | solution.py:24
  44.0 12.4 %collective-permute-start.1 = (bf16[2,576,128]{2,1,0:T(8,128)(2,1)}, bf16[2,576,128]{2,1,0:T(8,128)(2,1)}, u32[]{:S(2)}, u32[]{:S(2)}) collective-permute-start(bf16[2,576,128]{2,1,0:T(8,128)(2,1)} %bitcast.201), channel_id=1, source_target_pairs={{8,0},{16,8},{24,16},{32,24},{40,32},{48,40},{56,48},{64,56},{72,6... | collective-permute-start | bytes 884744 | tf_op jit(solution)/shard_map/ppermute | solution.py:27
  177.4 5.8 %copy-start.6 = (bf16[1024,128]{1,0:T(8,128)(2,1)S(1)}, bf16[1024,128]{1,0:T(8,128)(2,1)}, u32[]{:S(2)}) copy-start(bf16[1024,128]{1,0:T(8,128)(2,1)} %gather_fusion.4) | copy-start | bytes 786436
  177.4 5.8 %copy-start.7 = (f32[256,4]{1,0:T(8,128)S(1)}, f32[256,4]{1,0:T(8,128)}, u32[]{:S(2)}) copy-start(f32[256,4]{1,0:T(8,128)} %copy.170) | copy-start | bytes 12292
  177.4 6.2 %copy-start.5 = (bf16[1024,128]{1,0:T(8,128)(2,1)S(1)}, bf16[1024,128]{1,0:T(8,128)(2,1)}, u32[]{:S(2)}) copy-start(bf16[1024,128]{1,0:T(8,128)(2,1)} %gather_fusion.5) | copy-start | bytes 786436
  177.4 6.2 %copy-start.8 = (f32[256,4]{1,0:T(8,128)S(1)}, f32[256,4]{1,0:T(8,128)}, u32[]{:S(2)}) copy-start(f32[256,4]{1,0:T(8,128)} %copy.172) | copy-start | bytes 12292
  177.4 6.6 %copy-start.9 = (f32[256,4]{1,0:T(8,128)S(1)}, f32[256,4]{1,0:T(8,128)}, u32[]{:S(2)}) copy-start(f32[256,4]{1,0:T(8,128)} %copy.174) | copy-start | bytes 12292
  177.4 7.0 %copy-start.10 = (f32[256,4]{1,0:T(8,128)S(1)}, f32[256,4]{1,0:T(8,128)}, u32[]{:S(2)}) copy-start(f32[256,4]{1,0:T(8,128)} %copy.176) | copy-start | bytes 12292
  178.9 6.0 %copy-start.11 = (bf16[128,1024]{1,0:T(8,128)(2,1)S(1)}, bf16[128,1024]{1,0:T(8,128)(2,1)}, u32[]{:S(2)}) copy-start(bf16[128,1024]{1,0:T(8,128)(2,1)} %param.27) | copy-start | bytes 786436
  186.3 104.0 %all-gather.11.cloned.1.call-start = ((), (), s32[]{:S(2)}) async-start(), calls=%async_computation.5 | async-start | bytes 2752512 | tf_op jit(solution)/shard_map/all_gather | solution.py:54
  241.8 5.5 %copy-start.3 = (bf16[256,1024]{1,0:T(8,128)(2,1)S(1)}, bf16[256,1024]{1,0:T(8,128)(2,1)}, u32[]{:S(2)}) copy-start(bf16[256,1024]{1,0:T(8,128)(2,1)} %param.19) | copy-start | bytes 1572868
  247.3 11.1 %copy-start.14 = (f32[448]{0:T(512)S(1)}, f32[448]{0:T(512)}, u32[]{:S(2)}) copy-start(f32[448]{0:T(512)} %param.29) | copy-start | bytes 5380
  290.3 3.0 copy-start.18
  290.3 3.0 copy-start.20
  292.0 1.3 copy-start.4
  295.0 16.7 %copy-start.19 = (f32[384]{0:T(512)S(1)}, f32[384]{0:T(512)}, u32[]{:S(2)}) copy-start(f32[384]{0:T(512)} %param.31) | copy-start | bytes 4612
  295.0 14.8 %all-to-all-start.2 = ((bf16[8,256,128]{1,2,0:T(8,128)(2,1)}), bf16[8,256,128]{1,2,0:T(8,128)(2,1)S(1)}, u32[]{:S(2)}, u32[]{:S(2)}) async-start(bf16[8,256,128]{1,2,0:T(8,128)(2,1)} %broadcast_in_dim.124), calls=%async_computation.2 | async-start | bytes 1048576 | tf_op jit(solution)/shard_map/all_to_all | solution.py:38
  299.4 130.9 %all-gather.7.cloned.1.call-start = ((), (), s32[]{:S(2)}) async-start(), calls=%async_computation.3 | async-start | bytes 4456448 | tf_op jit(solution)/shard_map/all_gather | solution.py:71
  484.4 1.9 copy-start.1
Sparse Core Ops, SparseCore 0:
  186.4 55.3 all-gather.8
  275.0 15.2 all-gather.10
  310.7 119.5 all-gather.6
where the time goes:
time: 495 us; the launch traced here: 493 us
  waiting for transfers between devices  209 us (42%)
  local copies, waits for them, and re-layouts  165 us (33%)
  matrix products  36.9 us (7%)
  other arithmetic  28 us (6%)
  blocking collectives  22.6 us (5%)
  starting transfers between devices  16.1 us (3%)
  between operations  14.6 us (3%)
    gather x8, local copies, waits for them, and re-layouts, local(): picked = lookup[local_frame * patch_total + patch_id, head_lane]  119 us
    all_gather x1, waiting for transfers between devices, sent_together(): out, at, outs = (lax.all_gather(both, axis, axis=dim, tiled=True), 0, [])  114 us
    all_gather x1, waiting for transfers between devices, gathered_total(): return lax.all_gather(x, axis).sum(0)  55.3 us
    all_gather x1, waiting for transfers between devices, stacked_from(): parts = lax.all_gather(parts, axes[k])  15.4 us
    all_to_all x1, waiting for transfers between devices, local(): lax.all_to_all(projected, MP, split_axis=2, concat_axis=1, tiled=True)  14.6 us
    all_gather x1, blocking collectives, stacked_from(): parts = lax.all_gather(parts, axes[k])  14.3 us
    dot_general x8, matrix products, advance(): jnp.einsum('hqn,nhd->hqd', weights.astype(jnp.bfloat16), value_block, pre...  13.1 us
    dot_general x8, matrix products, advance(): jnp.einsum('qhd,nhd->hqn', query_turned, key_block, preferred_element_typ...  11.9 us
  transfers between devices with their start and end apart: 7, of which 5 were waited for; matrix products, arithmetic and copies ran while one was open for 4% of the time, Pallas kernels for 0%

commit v1 on v0

--- a/solution.py
+++ b/solution.py
@@ -1,3 +1,4 @@
+import functools
 import jax
 import jax.numpy as jnp
 from jax import lax
@@ -14,6 +15,21 @@
 rope_base = 1000000.0
 epsilon = 1e-06
 masked = -1e30
+
+
+def check_digits(local_values, ax_name, d_out, join_dim):
+    return jnp.concatenate(
+        lax.all_to_all(
+            jnp.stack(jnp.split(local_values, lax.axis_size(ax_name), axis=d_out)),
+            axis_name=ax_name,
+            split_axis=0,
+            concat_axis=0,
+        ),
+        axis=join_dim,
+    )
+
+
+sections_enter = functools.partial(check_digits, ax_name=MP, d_out=2, join_dim=1)
 
 
 def with_halo(block, sides, width):
@@ -211,7 +227,7 @@
     def own_slice(array):
         return lax.dynamic_slice_in_dim(array, group_index * heads_here, heads_here, 1)
 
-    by_head = lax.all_to_all(projected, MP, split_axis=2, concat_axis=1, tiled=True)
+    by_head = sections_enter(projected)
     padded = with_halo(by_head, (("tm", 0),), 2)
     lookup = padded.reshape(-1, heads_here, head_width)
     head_lane = jnp.arange(heads_here, dtype=jnp.int32)[None, :, None]

time: 495 us -> 516 us (1.042)
  other arithmetic: 28 us -> 41.6 us
  matrix products: 36.9 us -> 48.9 us
  waiting for transfers between devices: 209 us -> 203 us
    reduce_sum x8, other arithmetic: 2.48 us -> 13.7 us  [advance(): denominator = denominator * rescale + jnp.sum(weights, axis=-1)]
    dot_general x8, matrix products: 11.9 us -> 21 us  [advance(): jnp.einsum('qhd,nhd->hqn', query_turned, key_block, preferred_element_typ...]
    unnamed x47 -> x54, local copies, waits for them, and re-layouts: 5.67 us -> 10.4 us
  transfers between devices with their start and end apart: 7 -> 7, of which waited for: 5 -> 6; matrix products, arithmetic and copies ran while one was open for 4% -> 4% of each run, Pallas kernels for 0% -> 0%
where the time goes in v1:
time: 516 us; the launch traced here: 513 us
  waiting for transfers between devices  203 us (39%)
  local copies, waits for them, and re-layouts  166 us (32%)
  matrix products  48.9 us (9%)
  other arithmetic  41.6 us (8%)
  blocking collectives  22.6 us (4%)
  starting transfers between devices  15.7 us (3%)
  between operations  14.6 us (3%)
    gather x8, local copies, waits for them, and re-layouts, local(): picked = lookup[local_frame * patch_total + patch_id, head_lane]  119 us
    all_gather x1, waiting for transfers between devices, sent_together(): out, at, outs = (lax.all_gather(both, axis, axis=dim, tiled=True), 0, [])  110 us
    all_gather x1, waiting for transfers between devices, gathered_total(): return lax.all_gather(x, axis).sum(0)  55.5 us
    dot_general x8, matrix products, advance(): jnp.einsum('qhd,nhd->hqn', query_turned, key_block, preferred_element_typ...  21 us
    dot_general x8, matrix products, advance(): jnp.einsum('hqn,nhd->hqd', weights.astype(jnp.bfloat16), value_block, pre...  16.9 us
    all_gather x1, waiting for transfers between devices, stacked_from(): parts = lax.all_gather(parts, axes[k])  15.4 us
    all_gather x1, blocking collectives, stacked_from(): parts = lax.all_gather(parts, axes[k])  14.3 us
    reduce_sum x8, other arithmetic, advance(): denominator = denominator * rescale + jnp.sum(weights, axis=-1)  13.7 us
  transfers between devices with their start and end apart: 7, of which 6 were waited for; matrix products, arithmetic and copies ran while one was open for 4% of the time, Pallas kernels for 0%

profile of v1, /device:TPU:2, one launch (start us, length us, event | category | flops | bytes accessed | tf_op | source)
XLA Modules:
  0.0 513.3 jit_solution(10665661853371768038)
XLA Ops:
  7.2 2.7 convolution_convert_fusion
  15.2 4.5 all-to-all-start
  21.1 9.6 %all-to-all-done = bf16[8,4,72,128]{3,2,1,0:T(8,128)(2,1)} async-done(((bf16[8,4,72,128]{3,2,1,0:T(8,128)(2,1)}), bf16[8,4,72,128]{3,2,1,0:T(8,128)(2,1)}, u32[]{:S(2)}, u32[]{:S(2)}) %all-to-all-start) | async-done | bytes 589856 | tf_op jit(solution)/shard_map/all_to_all | solution.py:22
  32.8 3.8 collective-permute-start
  36.6 2.7 collective-permute-start.1
  52.1 16.0 %gather_fusion = bf16[1024,128]{1,0:T(8,128)(2,1)} fusion(bf16[4608,1,128]{2,0,1:T(8,128)(2,1)} %bitcast.198, s32[1024]{0:T(1024)S(1)} %reshape.435), kind=kCustom, calls=%fused_computation | custom fusion | bytes 532480 | tf_op jit(solution)/shard_map/gather | solution.py:244
  68.1 16.0 %gather_fusion.1 = bf16[1024,128]{1,0:T(8,128)(2,1)} fusion(bf16[4608,1,128]{2,0,1:T(8,128)(2,1)} %bitcast.199, s32[1024]{0:T(1024)S(1)} %reshape.443), kind=kCustom, calls=%fused_computation.1 | custom fusion | bytes 532480 | tf_op jit(solution)/shard_map/gather | solution.py:244
  84.0 16.0 %gather_fusion.2 = bf16[1024,128]{1,0:T(8,128)(2,1)} fusion(bf16[4608,1,128]{2,0,1:T(8,128)(2,1)} %bitcast.200, s32[1024]{0:T(1024)S(1)} %reshape.451), kind=kCustom, calls=%fused_computation.2 | custom fusion | bytes 532480 | tf_op jit(solution)/shard_map/gather | solution.py:244
  100.1 16.0 %gather_fusion.3 = bf16[1024,128]{1,0:T(8,128)(2,1)} fusion(bf16[4608,1,128]{2,0,1:T(8,128)(2,1)} %bitcast.201, s32[1024]{0:T(1024)S(1)} %reshape.459), kind=kCustom, calls=%fused_computation.3 | custom fusion | bytes 532480 | tf_op jit(solution)/shard_map/gather | solution.py:244
  116.1 15.9 %gather_fusion.4 = bf16[1024,128]{1,0:T(8,128)(2,1)} fusion(bf16[4608,1,128]{2,0,1:T(8,128)(2,1)} %bitcast.202, s32[1024]{0:T(1024)S(1)} %reshape.467), kind=kCustom, calls=%fused_computation.4 | custom fusion | bytes 532480 | tf_op jit(solution)/shard_map/gather | solution.py:244
  132.0 16.0 %gather_fusion.5 = bf16[1024,128]{1,0:T(8,128)(2,1)} fusion(bf16[4608,1,128]{2,0,1:T(8,128)(2,1)} %bitcast.203, s32[1024]{0:T(1024)S(1)} %reshape.475), kind=kCustom, calls=%fused_computation.5 | custom fusion | bytes 532480 | tf_op jit(solution)/shard_map/gather | solution.py:244
  148.0 11.4 %gather_fusion.6 = bf16[1024,128]{1,0:T(8,128)(2,1)S(1)} fusion(bf16[4608,1,128]{2,0,1:T(8,128)(2,1)} %bitcast.204, s32[1024]{0:T(1024)S(1)} %reshape.483), kind=kCustom, calls=%fused_computation.6 | custom fusion | bytes 532480 | tf_op jit(solution)/shard_map/gather | solution.py:244
  159.4 11.4 %gather_fusion.7 = bf16[1024,128]{1,0:T(8,128)(2,1)S(1)} fusion(bf16[4608,1,128]{2,0,1:T(8,128)(2,1)} %bitcast.205, s32[1024]{0:T(1024)S(1)} %reshape.491), kind=kCustom, calls=%fused_computation.7 | custom fusion | bytes 532480 | tf_op jit(solution)/shard_map/gather | solution.py:244
  180.0 55.5 %all-gather.9.cloned.1.call-done = f32[2048,1024]{1,0:T(8,128)} async-done(((f32[256,1024]{1,0:T(8,128)}), f32[2048,1024]{1,0:T(8,128)}) %all-gather.9.cloned.1.call-update) | async-done | bytes 8388624 | tf_op jit(solution)/shard_map/all_gather | solution.py:49
  235.5 5.5 %reduce_sum.126 = f32[256,1024]{1,0:T(8,128)} reduce(f32[8,256,1024]{2,1,0:T(8,128)} %bitcast.208, f32[]{:T(128)} %constant.44.clone.1), dimensions={0}, to_apply=%region_10.11 | reduce | flops 1835008 | bytes 9437188 | tf_op jit(solution)/shard_map/reduce_sum | solution.py:49
  241.0 2.7 multiply_reduce_fusion
  243.7 8.3 %all_to_all.16 = f32[8,1,256]{2,1,0:T(1,128)S(1)} all-to-all(f32[8,1,256]{2,1,0:T(1,128)S(1)} %broadcast_in_dim.123), channel_id=1, replica_groups=mesh['dp'=2,'tm'=16,'mp_0'=4,'mp_1'=2] {'mp_0','mp_1'}, dimensions={0} | all-to-all | bytes 16384 | tf_op jit(solution)/shard_map/all_to_all | solution.py:54
  253.2 14.3 %all-gather.1 = bf16[1024,448]{0,1:T(8,128)(2,1)S(1)} all-gather(bf16[256,448]{0,1:T(8,128)(2,1)S(1)} %multiply_convert_fusion), channel_id=3, replica_groups=mesh['dp'=2,'tm'=16,'mp_0'=4,'mp_1'=2] {'mp_0'}, dimensions={0}, use_global_device_ids=true | all-gather | bytes 1146880 | tf_op jit(solution)/shard_map/all_gather | solution.py:70
  268.5 15.4 %all-gather.11.cloned.1.call-done = bf16[8,256,448]{1,2,0:T(8,128)(2,1)} async-done(((bf16[4,256,448]{1,2,0:T(8,128)(2,1)}), bf16[8,256,448]{1,2,0:T(8,128)(2,1)}) %all-gather.11.cloned.1.call-update) | async-done | bytes 1835024 | tf_op jit(solution)/shard_map/all_gather | solution.py:70
  288.6 4.4 all-to-all-start.2
  293.1 10.3 %all-to-all-done.2 = bf16[8,256,128]{1,2,0:T(8,128)(2,1)S(1)} async-done(((bf16[8,256,128]{1,2,0:T(8,128)(2,1)}), bf16[8,256,128]{1,2,0:T(8,128)(2,1)S(1)}, u32[]{:S(2)}, u32[]{:S(2)}) %all-to-all-start.2) | async-done | bytes 524320 | tf_op jit(solution)/shard_map/all_to_all | solution.py:54
  305.3 3.4 convolution_add_fusion.1
  313.5 110.3 %all-gather.7.cloned.1.call-done = bf16[4096,512]{0,1:T(8,128)(2,1)} async-done(((bf16[256,512]{0,1:T(8,128)(2,1)}), bf16[4096,512]{0,1:T(8,128)(2,1)}) %all-gather.7.cloned.1.call-update) | async-done | bytes 4194320 | tf_op jit(solution)/shard_map/all_gather | solution.py:87
  423.9 2.7 fusion.82
  432.5 4.1 gather_fusion.9
  436.6 4.1 gather_fusion.8
  440.7 63.3 %while.15 = (s32[]{:T(128)}, f32[3,256]{1,0:T(4,128)S(1)}, f32[3,256]{1,0:T(4,128)S(1)}, f32[3,256,128]{2,1,0:T(8,128)S(1)}, s32[8]{0:T(128)S(1)}, /*index=5*/bf...) while((s32[]{:T(128)}, f32[3,256]{1,0:T(4,128)S(1)}, ...), condition=%wide.region_16.17_spmd.clone, body=%wide.region_13.16_spmd.clone.sunk | while | flops 205296128 | bytes 7068813 | solution.py:181
  450.0 2.6 fusion.106
  457.9 2.6 fusion.106
  465.9 2.6 fusion.106
  489.6 2.6 fusion.106
  497.5 2.6 fusion.106
  (229 shorter events, 102.1 us)
Async XLA Ops:
  7.2 298.2 %copy-start = (bf16[3584,384]{1,0:T(8,128)(2,1)S(1)}, bf16[3584,384]{1,0:T(8,128)(2,1)}, u32[]{:S(2)}) copy-start(bf16[3584,384]{1,0:T(8,128)(2,1)} %param.30) | copy-start | bytes 8257540
  9.9 9.8 %copy-start.1 = (bf16[256,1024]{1,0:T(8,128)(2,1)S(1)}, bf16[256,1024]{1,0:T(8,128)(2,1)}, u32[]{:S(2)}) copy-start(bf16[256,1024]{1,0:T(8,128)(2,1)} %param.19) | copy-start | bytes 1572868
  9.9 9.8 %copy-start.13 = (bf16[1024,32]{0,1:T(8,128)(2,1)S(1)}, bf16[1024,32]{0,1:T(8,128)(2,1)}, u32[]{:S(2)}) copy-start(bf16[1024,32]{0,1:T(8,128)(2,1)} %param.25) | copy-start | bytes 196612
  9.9 9.8 %copy-start.17 = (f32[32]{0:T(128)S(1)}, f32[32]{0:T(128)}, u32[]{:S(2)}) copy-start(f32[32]{0:T(128)} %param.26) | copy-start | bytes 388
  9.9 10.1 %copy-start.12 = (f32[2,256,8,4]{1,3,2,0:T(4,128)S(1)}, f32[2,256,8,4]{1,3,2,0:T(4,128)}, u32[]{:S(2)}) copy-start(f32[2,256,8,4]{1,3,2,0:T(4,128)} %param.23) | copy-start | bytes 196612
  9.9 10.2 %copy-start.15 = (s32[256]{0:T(256)S(1)}, s32[256]{0:T(256)}, u32[]{:S(2)}) copy-start(s32[256]{0:T(256)} %param.21) | copy-start | bytes 3076
  9.9 10.2 %copy-start.16 = (s32[256]{0:T(256)S(1)}, s32[256]{0:T(256)}, u32[]{:S(2)}) copy-start(s32[256]{0:T(256)} %param.20) | copy-start | bytes 3076
  15.2 15.6 %all-to-all-start = ((bf16[8,4,72,128]{3,2,1,0:T(8,128)(2,1)}), bf16[8,4,72,128]{3,2,1,0:T(8,128)(2,1)}, u32[]{:S(2)}, u32[]{:S(2)}) async-start(bf16[8,4,72,128]{3,2,1,0:T(8,128)(2,1)} %fusion.30), calls=%async_computation | async-start | bytes 1179648 | tf_op jit(solution)/shard_map/all_to_all | solution.py:22
  19.6 215.9 %all-gather.9.cloned.1.call-start = ((), (), s32[]{:S(2)}) async-start(), calls=%async_computation.4 | async-start | bytes 9437184 | tf_op jit(solution)/shard_map/all_gather | solution.py:49
  32.8 17.1 %collective-permute-start = (bf16[2,576,128]{2,1,0:T(8,128)(2,1)}, bf16[2,576,128]{2,1,0:T(8,128)(2,1)}, u32[]{:S(2)}, u32[]{:S(2)}) collective-permute-start(bf16[2,576,128]{2,1,0:T(8,128)(2,1)} %bitcast.14), channel_id=1, source_target_pairs={{0,8},{8,16},{16,24},{24,32},{32,40},{40,48},{48,56},{56,64},{64,7... | collective-permute-start | bytes 884744 | tf_op jit(solution)/shard_map/ppermute | solution.py:40
  36.6 13.3 %collective-permute-start.1 = (bf16[2,576,128]{2,1,0:T(8,128)(2,1)}, bf16[2,576,128]{2,1,0:T(8,128)(2,1)}, u32[]{:S(2)}, u32[]{:S(2)}) collective-permute-start(bf16[2,576,128]{2,1,0:T(8,128)(2,1)} %bitcast.16), channel_id=1, source_target_pairs={{8,0},{16,8},{24,16},{32,24},{40,32},{48,40},{56,48},{64,56},{72,6... | collective-permute-start | bytes 884744 | tf_op jit(solution)/shard_map/ppermute | solution.py:43
  159.4 11.5 %copy-start.6 = (f32[256,4]{1,0:T(8,128)S(1)}, f32[256,4]{1,0:T(8,128)}, u32[]{:S(2)}) copy-start(f32[256,4]{1,0:T(8,128)} %copy.157) | copy-start | bytes 12292
  170.8 5.8 %copy-start.5 = (bf16[1024,128]{1,0:T(8,128)(2,1)S(1)}, bf16[1024,128]{1,0:T(8,128)(2,1)}, u32[]{:S(2)}) copy-start(bf16[1024,128]{1,0:T(8,128)(2,1)} %gather_fusion.4) | copy-start | bytes 786436
  170.8 5.8 %copy-start.7 = (f32[256,4]{1,0:T(8,128)S(1)}, f32[256,4]{1,0:T(8,128)}, u32[]{:S(2)}) copy-start(f32[256,4]{1,0:T(8,128)} %copy.166) | copy-start | bytes 12292
  170.8 6.2 %copy-start.4 = (bf16[1024,128]{1,0:T(8,128)(2,1)S(1)}, bf16[1024,128]{1,0:T(8,128)(2,1)}, u32[]{:S(2)}) copy-start(bf16[1024,128]{1,0:T(8,128)(2,1)} %gather_fusion.5) | copy-start | bytes 786436
  170.8 6.2 %copy-start.8 = (f32[256,4]{1,0:T(8,128)S(1)}, f32[256,4]{1,0:T(8,128)}, u32[]{:S(2)}) copy-start(f32[256,4]{1,0:T(8,128)} %copy.168) | copy-start | bytes 12292
  170.9 6.6 %copy-start.9 = (f32[256,4]{1,0:T(8,128)S(1)}, f32[256,4]{1,0:T(8,128)}, u32[]{:S(2)}) copy-start(f32[256,4]{1,0:T(8,128)} %copy.170) | copy-start | bytes 12292
  170.9 7.0 %copy-start.10 = (f32[256,4]{1,0:T(8,128)S(1)}, f32[256,4]{1,0:T(8,128)}, u32[]{:S(2)}) copy-start(f32[256,4]{1,0:T(8,128)} %copy.172) | copy-start | bytes 12292
  172.3 6.0 %copy-start.11 = (bf16[128,1024]{1,0:T(8,128)(2,1)S(1)}, bf16[128,1024]{1,0:T(8,128)(2,1)}, u32[]{:S(2)}) copy-start(bf16[128,1024]{1,0:T(8,128)(2,1)} %param.27) | copy-start | bytes 786436
  179.7 104.2 %all-gather.11.cloned.1.call-start = ((), (), s32[]{:S(2)}) async-start(), calls=%async_computation.5 | async-start | bytes 2752512 | tf_op jit(solution)/shard_map/all_gather | solution.py:70
  235.5 5.5 %copy-start.2 = (bf16[256,1024]{1,0:T(8,128)(2,1)S(1)}, bf16[256,1024]{1,0:T(8,128)(2,1)}, u32[]{:S(2)}) copy-start(bf16[256,1024]{1,0:T(8,128)(2,1)} %param.19) | copy-start | bytes 1572868
  241.0 11.1 %copy-start.14 = (f32[448]{0:T(512)S(1)}, f32[448]{0:T(512)}, u32[]{:S(2)}) copy-start(f32[448]{0:T(512)} %param.29) | copy-start | bytes 5380
  283.9 3.0 copy-start.18
  283.9 3.0 copy-start.20
  285.6 1.3 copy-start.3
  288.6 16.7 %copy-start.19 = (f32[384]{0:T(512)S(1)}, f32[384]{0:T(512)}, u32[]{:S(2)}) copy-start(f32[384]{0:T(512)} %param.31) | copy-start | bytes 4612
  288.6 14.8 %all-to-all-start.2 = ((bf16[8,256,128]{1,2,0:T(8,128)(2,1)}), bf16[8,256,128]{1,2,0:T(8,128)(2,1)S(1)}, u32[]{:S(2)}, u32[]{:S(2)}) async-start(bf16[8,256,128]{1,2,0:T(8,128)(2,1)} %broadcast_in_dim.124), calls=%async_computation.2 | async-start | bytes 1048576 | tf_op jit(solution)/shard_map/all_to_all | solution.py:54
  293.0 130.9 %all-gather.7.cloned.1.call-start = ((), (), s32[]{:S(2)}) async-start(), calls=%async_computation.3 | async-start | bytes 4456448 | tf_op jit(solution)/shard_map/all_gather | solution.py:87
Sparse Core Ops, SparseCore 0:
  179.8 55.5 all-gather.8
  268.6 15.2 all-gather.10
  304.3 119.5 all-gather.6
